TPU v7x, 128 devices: a whole 4x4x4 slice. The times are simulated.
128 devices in a mesh: row: 8 (over z, y_lo), col: 16 (over x, y_hi, core).
Axes of the slice: x: 4, y: 4 (y_hi: 2, y_lo: 2; y = y_hi * 2 + y_lo), z: 4, core: 2. Of those that a mesh axis runs over, the one named last changes fastest.
Arguments:
- seq_ids: int32 [4096], replicated, may hold values from 0 to 31, never falling along the last dimension, each value on 1 to 192 neighbouring positions
- attn_weights: float32 [4096, 64, 32], P(('row', 'col')), may hold values from 0.05 to 20
- values: bfloat16 [4096, 8192], P(('row', 'col')), may hold values from -6 to 6
- out_grads: bfloat16 [4096, 8192], P(('row', 'col')), may hold values from -2 to 2
- act_basis: bfloat16 [8192, 8192], P('row', 'col'), may hold values from -0.0625 to 0.0625
- grad_basis: bfloat16 [8192, 8192], P('col', 'row'), may hold values from -0.0625 to 0.0625
Outputs:
- eigenvalues: float32 [8192, 8192], P('row', 'col')
Inputs may be any that keep to these rules, and one draw needn't show every extreme that they name: `seq_ids`: ids never fall along the tokens; each of the 32 sequences is one run of 1 to 192 tokens, and one has exactly 192.
All inputs are finite; a program needn't handle non-finite values.
Results may differ from a plain program's by a relative error of at most 0.014.
Values may be sent and summed in bfloat16 or wider, within the bound.
No kernel may reach another device: no remote copies, remote signals or barrier semaphores. Data moves between devices by JAX's collectives and lax.ppermute only.
A program may use at most 128 MiB of HBM per device.

v0:
```python
import jax
import jax.numpy as jnp
from jax import lax
from jax.sharding import PartitionSpec as P

SEQ_MEAN = 128
LONGEST = 192


def from_behind(value, axis, steps):
    count = lax.axis_size(axis)
    initial, last = (max(0, -steps), min(count, count - steps))
    return lax.ppermute(value, axis, [(source, source + steps) for source in range(initial, last)])


def shards(seq_ids, attn_weights, values, out_grads, act_basis, grad_basis):
    tok = values.shape[0]
    width = values.shape[1]
    heads = attn_weights.shape[1]
    window = attn_weights.shape[2]
    head_size = width // heads
    total_tok = seq_ids.shape[0]
    offset = lax.axis_index(("row", "col")) * tok
    previous = from_behind(values, ("row", "col"), 1)
    keys = jnp.concatenate([previous, values], axis=0).reshape(2 * tok, heads, head_size)
    query_pos = offset + jnp.arange(tok, dtype=jnp.int32)
    steps_back = jnp.arange(window, dtype=jnp.int32)
    key_pos = query_pos[:, None] - steps_back[None, :]
    key_seg = jnp.take(seq_ids, jnp.clip(key_pos, 0, total_tok - 1))
    query_seg = lax.dynamic_slice_in_dim(seq_ids, offset, tok, 0)
    valid = jnp.logical_and(key_pos >= 0, key_seg == query_seg[:, None]).astype(jnp.float32)
    masked = attn_weights * valid[:, None, :]
    probs = (masked / jnp.sum(masked, axis=2, keepdims=True)).astype(jnp.bfloat16)
    local_key = tok + jnp.arange(tok, dtype=jnp.int32)[:, None] - steps_back[None, :]
    selector = (
        local_key[:, :, None] == jnp.arange(2 * tok, dtype=jnp.int32)[None, None, :]
    ).astype(jnp.bfloat16)
    spread = jnp.einsum("phj,pjk->phk", probs, selector, preferred_element_type=jnp.float32).astype(
        jnp.bfloat16
    )
    mixed = jnp.einsum("phk,khd->phd", spread, keys, preferred_element_type=jnp.float32)
    inputs = mixed.reshape(tok, width).astype(jnp.bfloat16)
    col_tokens = lax.all_gather(inputs, "col", axis=0, tiled=True)
    act_rows = lax.all_to_all(col_tokens, "row", split_axis=1, concat_axis=0, tiled=True)
    grad_cols = lax.all_to_all(out_grads, "col", split_axis=1, concat_axis=0, tiled=True)
    act_part = jnp.dot(act_rows, act_basis, preferred_element_type=jnp.float32)
    rot_inputs = lax.psum(act_part.astype(jnp.bfloat16), "row")
    grad_part = jnp.dot(
        lax.all_gather(grad_cols, "row", axis=0, tiled=True),
        grad_basis,
        preferred_element_type=jnp.float32,
    )
    rot_grads = lax.psum(grad_part.astype(jnp.bfloat16), "col")
    sequences = total_tok // SEQ_MEAN
    seq_range = jnp.arange(sequences, dtype=jnp.int32)
    starts = jnp.sum((seq_ids[None, :] < seq_range[:, None]).astype(jnp.int32), axis=1)

    def accumulate(index, running):
        first = jnp.minimum(starts[index], total_tok - LONGEST)
        grad_win = lax.dynamic_slice_in_dim(rot_grads, first, LONGEST, 0)
        act_win = lax.dynamic_slice_in_dim(rot_inputs, first, LONGEST, 0)
        seg_win = lax.dynamic_slice_in_dim(seq_ids, first, LONGEST, 0)
        grad_win = jnp.where((seg_win == index)[:, None], grad_win, jnp.zeros_like(grad_win))
        tile = lax.dot_general(
            grad_win, act_win, (((0,), (0,)), ((), ())), preferred_element_type=jnp.float32
        )
        return running + tile * tile

    start_acc = jnp.zeros((rot_grads.shape[1], rot_inputs.shape[1]), jnp.float32)
    running = lax.fori_loop(0, sequences, accumulate, start_acc)
    return running / sequences


def solution(mesh):
    return jax.shard_map(
        shards,
        mesh=mesh,
        in_specs=(
            P(),
            P(("row", "col"), None, None),
            P(("row", "col"), None),
            P(("row", "col"), None),
            P("row", "col"),
            P("col", "row"),
        ),
        out_specs=P("row", "col"),
        check_vma=False,
    )
```

profile of v0, /device:TPU:1, one launch (start us, length us, event | category | flops | bytes accessed | tf_op | source)
XLA Modules:
  0.0 764.4 jit_solution(13722554175715959616)
XLA Ops:
  6.5 6.3 collective-permute-start
  13.8 6.1 gather_fusion
  22.9 17.1 %all_to_all.38 = bf16[32,16,512]{2,0,1:T(8,128)(2,1)} all-to-all(bf16[32,16,512]{2,0,1:T(8,128)(2,1)S(1)} %bitcast.40), channel_id=1, replica_groups=mesh['row'=8,'col'=16] {'col'}, dimensions={1} | all-to-all | bytes 1048576 | tf_op jit(solution)/shard_map/all_to_all | solution.py:45
  40.0 56.9 %all-gather.5.cloned.1.call-done = bf16[512,8192]{1,0:T(8,128)(2,1)} async-done(((bf16[32,8192]{1,0:T(8,128)(2,1)}), bf16[512,8192]{1,0:T(8,128)(2,1)}) %all-gather.5.cloned.1.call-update) | async-done | bytes 8388624 | tf_op jit(solution)/shard_map/all_gather | solution.py:43
  97.0 8.0 %copy.38 = bf16[64,8,8,1024]{3,2,0,1:T(8,128)(2,1)} copy(bf16[64,8,8,1024]{3,2,1,0:T(8,128)(2,1)} %bitcast.37) | data formatting | bytes 16777216 | tf_op jit(solution)/shard_map/all_to_all | solution.py:44
  105.0 5.0 all-to-all-start.1
  110.1 147.4 %all-gather.3.cloned.1.call-done = bf16[4096,512]{1,0:T(8,128)(2,1)} async-done(((bf16[512,512]{1,0:T(8,128)(2,1)}), bf16[4096,512]{1,0:T(8,128)(2,1)}) %all-gather.3.cloned.1.call-update) | async-done | bytes 4194320 | tf_op jit(solution)/shard_map/all_gather | solution.py:49
  257.5 9.0 %convolution_convert_fusion = bf16[4096,1024]{1,0:T(8,128)(2,1)} fusion(bf16[4096,512]{1,0:T(8,128)(2,1)} %all-gather.3.cloned.1.call-done, bf16[512,1024]{1,0:T(8,128)(2,1)S(1)} %copy-done), kind=kOutput, calls=%fused_computation.11 | convolution fusion | flops 4299161600 | bytes 13631488 | tf_op jit(solution)/shard_map/dot_general | solution.py:48
  266.6 11.0 %all-to-all-done.1 = bf16[512,8,1024]{2,0,1:T(8,128)(2,1)} async-done(((bf16[512,8,1024]{2,0,1:T(8,128)(2,1)}), bf16[512,8,1024]{2,0,1:T(8,128)(2,1)}, u32[]{:S(2)}, u32[]{:S(2)}) %all-to-all-start.1) | async-done | bytes 8388640 | tf_op jit(solution)/shard_map/all_to_all | solution.py:44
  277.6 9.5 %convolution_convert_fusion.1 = bf16[4096,512]{1,0:T(8,128)(2,1)} fusion(bf16[4096,1024]{1,0:T(8,128)(2,1)} %bitcast.4, bf16[1024,512]{1,0:T(8,128)(2,1)S(1)} %copy-done.4), kind=kOutput, calls=%fused_computation.12 | convolution fusion | flops 4297064448 | bytes 13631488 | tf_op jit(solution)/shard_map/dot_general | solution.py:46
  287.3 185.7 %all-reduce.3.cloned.1.call-done = bf16[4096,1024]{1,0:T(8,128)(2,1)} async-done(((bf16[4096,1024]{1,0:T(8,128)(2,1)}), bf16[4096,1024]{1,0:T(8,128)(2,1)}) %all-reduce.3.cloned.1.call-update) | async-done | bytes 8388624 | tf_op jit(solution)/shard_map/psum | solution.py:53
  473.0 184.0 %all-reduce.5.cloned.1.call-done = bf16[4096,512]{1,0:T(8,128)(2,1)} async-done(((bf16[4096,512]{1,0:T(8,128)(2,1)}), bf16[4096,512]{1,0:T(8,128)(2,1)}) %all-reduce.5.cloned.1.call-update) | async-done | bytes 4194320 | tf_op jit(solution)/shard_map/psum | solution.py:47
  657.0 99.3 %while.14 = (s32[]{:T(128)}, f32[1024,512]{1,0:T(8,128)S(1)}, s32[32]{0:T(128)S(1)}, s32[4096]{0:T(1024)S(1)}, bf16[4096,1024]{1,0:T(8,128)(2,1)}, /*index=5*/bf...) while((s32[]{:T(128)}, f32[1024,512]{1,0:T(8,128)S(1)}, ...), condition=%wide.region_5.6_spmd.clone, body=%wide.region_4.5_spmd.clone.sunk | while | flops 203096256 | bytes 4786992 | solution.py:70
  658.2 1.9 select_add_fusion.2
  661.3 1.9 select_add_fusion.2
  667.5 1.9 select_add_fusion.2
  670.6 1.9 select_add_fusion.2
  676.8 1.9 select_add_fusion.2
  683.1 1.9 select_add_fusion.2
  686.2 1.9 select_add_fusion.2
  692.4 1.9 select_add_fusion.2
  698.6 1.9 select_add_fusion.2
  701.7 1.9 select_add_fusion.2
  707.9 1.9 select_add_fusion.2
  714.1 1.9 select_add_fusion.2
  717.2 1.9 select_add_fusion.2
  723.4 1.9 select_add_fusion.2
  729.6 1.9 select_add_fusion.2
  732.7 1.9 select_add_fusion.2
  738.9 1.9 select_add_fusion.2
  745.1 1.9 select_add_fusion.2
  748.2 1.9 select_add_fusion.2
  (115 shorter events, 50.6 us)
Async XLA Ops:
  6.5 251.0 %copy-start = (bf16[512,1024]{1,0:T(8,128)(2,1)S(1)}, bf16[512,1024]{1,0:T(8,128)(2,1)}, u32[]{:S(2)}) copy-start(bf16[512,1024]{1,0:T(8,128)(2,1)} %param.13) | copy-start | bytes 3145732
  6.5 7.3 copy-start.1
  6.5 90.4 %all-gather.5.cloned.1.call-start = ((), (), s32[]{:S(2)}) async-start(), calls=%async_computation.4 | async-start | bytes 8912896 | tf_op jit(solution)/shard_map/all_gather | solution.py:43
  6.5 14.8 %collective-permute-start = (bf16[32,8192]{1,0:T(8,128)(2,1)}, bf16[32,8192]{1,0:T(8,128)(2,1)S(1)}, u32[]{:S(2)}, u32[]{:S(2)}) collective-permute-start(bf16[32,8192]{1,0:T(8,128)(2,1)} %param.10), channel_id=1, source_target_pairs={{0,1},{1,2},{2,3},{3,4},{4,5},{5,6},{6,7},{7,8},{8,9},{9,10},{10,1... | collective-permute-start | bytes 1572872 | tf_op jit(solution)/shard_map/ppermute | solution.py:13
  13.8 6.3 copy-start.2
  13.8 7.5 copy-start.5
  20.0 2.9 copy-start.3
  22.8 234.7 %all-gather.3.cloned.1.call-start = ((), (), s32[]{:S(2)}) async-start(), calls=%async_computation.2 | async-start | bytes 4718592 | tf_op jit(solution)/shard_map/all_gather | solution.py:49
  105.0 172.6 %all-to-all-start.1 = ((bf16[512,8,1024]{2,0,1:T(8,128)(2,1)}), bf16[512,8,1024]{2,0,1:T(8,128)(2,1)}, u32[]{:S(2)}, u32[]{:S(2)}) async-start(bf16[512,8,1024]{2,0,1:T(8,128)(2,1)} %bitcast.36), calls=%async_computation.1 | async-start | bytes 16777216 | tf_op jit(solution)/shard_map/all_to_all | solution.py:44
  110.0 363.0 %all-reduce.3.cloned.1.call-start = ((), (), s32[]{:S(2)}) async-start(), calls=%async_computation.3 | async-start | bytes 16777216 | tf_op jit(solution)/shard_map/psum | solution.py:53
  266.5 11.1 %copy-start.4 = (bf16[1024,512]{1,0:T(8,128)(2,1)S(1)}, bf16[1024,512]{1,0:T(8,128)(2,1)}, u32[]{:S(2)}) copy-start(bf16[1024,512]{1,0:T(8,128)(2,1)} %param.12) | copy-start | bytes 3145732
  266.5 390.5 %all-reduce.5.cloned.1.call-start = ((), (), s32[]{:S(2)}) async-start(), calls=%async_computation.5 | async-start | bytes 8388608 | tf_op jit(solution)/shard_map/psum | solution.py:47
Sparse Core Ops, SparseCore 0:
  22.9 73.9 all-gather.4
  98.6 158.8 all-gather.2
  266.6 206.3 all-reduce.2
  475.4 181.5 all-reduce.4
where the time goes:
time: 766 us; the launch traced here: 764 us
  waiting for transfers between devices  585 us (76%)
  matrix products  80 us (10%)
  local copies, waits for them, and re-layouts  33.9 us (4%)
  loops' own time  18.7 us (2%)
  blocking collectives  17.1 us (2%)
  between operations  13.3 us (2%)
  starting transfers between devices  11.5 us (2%)
    psum x1, waiting for transfers between devices, shards(): rot_grads = lax.psum(grad_part.astype(jnp.bfloat16), 'col')  186 us
    psum x1, waiting for transfers between devices, shards(): rot_inputs = lax.psum(act_part.astype(jnp.bfloat16), 'row')  184 us
    all_gather x1, waiting for transfers between devices, shards(): lax.all_gather(grad_cols, 'row', axis=0, tiled=True)  147 us
    dot_general x32, matrix products, accumulate(): lax.dot_general(grad_win, act_win, (((0,), (0,)), ((), ())), preferred_el...  60.1 us
    all_gather x1, waiting for transfers between devices, shards(): col_tokens = lax.all_gather(inputs, 'col', axis=0, tiled=True)  56.9 us
    another operation x1, loops' own time, shards(): running = lax.fori_loop(0, sequences, accumulate, start_acc)  18.7 us
    dynamic_slice x32, local copies, waits for them, and re-layouts, accumulate(): first = jnp.minimum(starts[index], total_tok - LONGEST)  17.9 us
    all_to_all x1, blocking collectives, shards(): lax.all_to_all(out_grads, 'col', split_axis=1, concat_axis=0, tiled=True)  17.1 us
  transfers between devices with their start and end apart: 6, of which 5 were waited for; matrix products, arithmetic and copies ran while one was open for 5% of the time, Pallas kernels for 0%

commit v1 on v0

--- a/solution.py
+++ b/solution.py
@@ -46,7 +46,9 @@
     act_part = jnp.dot(act_rows, act_basis, preferred_element_type=jnp.float32)
     rot_inputs = lax.psum(act_part.astype(jnp.bfloat16), "row")
     grad_part = jnp.dot(
-        lax.all_gather(grad_cols, "row", axis=0, tiled=True),
+        jnp.concatenate(
+            lax.all_to_all(jnp.stack([grad_cols] * lax.axis_size("row")), "row", 0, 0), axis=0
+        ),
         grad_basis,
         preferred_element_type=jnp.float32,
     )

time: 766 us -> 709 us (0.926)
  waiting for transfers between devices: 585 us -> 515 us
    all_to_all x1, waiting for transfers between devices: 11 us -> 163 us  [shards(): lax.all_to_all(col_tokens, 'row', split_axis=1, concat_axis=0, tiled=True)]
    all_gather x1 -> x0, waiting for transfers between devices: 147 us -> none  [shards(): lax.all_gather(grad_cols, 'row', axis=0, tiled=True)]
    psum x1, waiting for transfers between devices: 186 us -> 96.5 us  [shards(): rot_grads = lax.psum(grad_part.astype(jnp.bfloat16), 'col')]
    all_gather x1, waiting for transfers between devices: 56.9 us -> 71.7 us  [shards(): col_tokens = lax.all_gather(inputs, 'col', axis=0, tiled=True)]
  transfers between devices with their start and end apart: 6 -> 6, of which waited for: 5 -> 4; matrix products, arithmetic and copies ran while one was open for 5% -> 5% of each run, Pallas kernels for 0% -> 0%
where the time goes in v1:
time: 709 us; the launch traced here: 707 us
  waiting for transfers between devices  515 us (73%)
  matrix products  80 us (11%)
  local copies, waits for them, and re-layouts  38.9 us (5%)
  loops' own time  20.9 us (3%)
  starting transfers between devices  17.2 us (2%)
  blocking collectives  17 us (2%)
  between operations  13.3 us (2%)
    psum x1, waiting for transfers between devices, shards(): rot_inputs = lax.psum(act_part.astype(jnp.bfloat16), 'row')  184 us
    all_to_all x1, waiting for transfers between devices, shards(): lax.all_to_all(col_tokens, 'row', split_axis=1, concat_axis=0, tiled=True)  163 us
    psum x1, waiting for transfers between devices, shards(): rot_grads = lax.psum(grad_part.astype(jnp.bfloat16), 'col')  96.5 us
    all_gather x1, waiting for transfers between devices, shards(): col_tokens = lax.all_gather(inputs, 'col', axis=0, tiled=True)  71.7 us
    dot_general x32, matrix products, accumulate(): lax.dot_general(grad_win, act_win, (((0,), (0,)), ((), ())), preferred_el...  60.1 us
    another operation x1, loops' own time, shards(): running = lax.fori_loop(0, sequences, accumulate, start_acc)  20.9 us
    dynamic_slice x32, local copies, waits for them, and re-layouts, accumulate(): first = jnp.minimum(starts[index], total_tok - LONGEST)  20.5 us
    all_to_all x1, blocking collectives, shards(): lax.all_to_all(out_grads, 'col', split_axis=1, concat_axis=0, tiled=True)  17 us
  transfers between devices with their start and end apart: 6, of which 4 were waited for; matrix products, arithmetic and copies ran while one was open for 5% of the time, Pallas kernels for 0%

profile of v1, /device:TPU:1, one launch (start us, length us, event | category | flops | bytes accessed | tf_op | source)
XLA Modules:
  0.0 707.1 jit_solution(2274060817579303788)
XLA Ops:
  6.5 6.3 collective-permute-start
  13.8 6.1 gather_fusion
  22.9 17.0 %all_to_all.40 = bf16[32,16,512]{2,0,1:T(8,128)(2,1)S(1)} all-to-all(bf16[32,16,512]{2,0,1:T(8,128)(2,1)S(1)} %bitcast.41), channel_id=1, replica_groups=mesh['row'=8,'col'=16] {'col'}, dimensions={1} | all-to-all | bytes 1048576 | tf_op jit(solution)/shard_map/all_to_all | solution.py:45
  39.9 2.3 stack.5
  42.2 5.8 all-to-all-start.1
  48.0 71.7 %all-gather.2.cloned.1.call-done = bf16[512,8192]{1,0:T(8,128)(2,1)} async-done(((bf16[32,8192]{1,0:T(8,128)(2,1)}), bf16[512,8192]{1,0:T(8,128)(2,1)}) %all-gather.2.cloned.1.call-update) | async-done | bytes 8388624 | tf_op jit(solution)/shard_map/all_gather | solution.py:43
  119.7 8.0 %copy.38 = bf16[64,8,8,1024]{3,2,0,1:T(8,128)(2,1)} copy(bf16[64,8,8,1024]{3,2,1,0:T(8,128)(2,1)} %bitcast.38) | data formatting | bytes 16777216 | tf_op jit(solution)/shard_map/all_to_all | solution.py:44
  127.7 5.0 all-to-all-start.2
  132.8 8.9 %convolution_convert_fusion = bf16[4096,1024]{1,0:T(8,128)(2,1)} fusion(bf16[4096,512]{1,0:T(8,128)(2,1)} %bitcast.2, bf16[512,1024]{1,0:T(8,128)(2,1)S(1)} %copy-done), kind=kOutput, calls=%fused_computation.11 | convolution fusion | flops 4299161600 | bytes 13631488 | tf_op jit(solution)/shard_map/dot_general | solution.py:48
  141.8 162.7 %all-to-all-done.2 = bf16[512,8,1024]{2,0,1:T(8,128)(2,1)} async-done(((bf16[512,8,1024]{2,0,1:T(8,128)(2,1)}), bf16[512,8,1024]{2,0,1:T(8,128)(2,1)}, u32[]{:S(2)}, u32[]{:S(2)}) %all-to-all-start.2) | async-done | bytes 8388640 | tf_op jit(solution)/shard_map/all_to_all | solution.py:44
  304.5 9.6 %convolution_convert_fusion.1 = bf16[4096,512]{1,0:T(8,128)(2,1)} fusion(bf16[4096,1024]{1,0:T(8,128)(2,1)} %bitcast.5, bf16[1024,512]{1,0:T(8,128)(2,1)S(1)} %copy-done.5), kind=kOutput, calls=%fused_computation.12 | convolution fusion | flops 4297064448 | bytes 13631488 | tf_op jit(solution)/shard_map/dot_general | solution.py:46
  314.3 96.5 %all-reduce.3.cloned.1.call-done = bf16[4096,1024]{1,0:T(8,128)(2,1)} async-done(((bf16[4096,1024]{1,0:T(8,128)(2,1)}), bf16[4096,1024]{1,0:T(8,128)(2,1)}) %all-reduce.3.cloned.1.call-update) | async-done | bytes 8388624 | tf_op jit(solution)/shard_map/psum | solution.py:55
  410.8 184.1 %all-reduce.5.cloned.1.call-done = bf16[4096,512]{1,0:T(8,128)(2,1)} async-done(((bf16[4096,512]{1,0:T(8,128)(2,1)}), bf16[4096,512]{1,0:T(8,128)(2,1)}) %all-reduce.5.cloned.1.call-update) | async-done | bytes 4194320 | tf_op jit(solution)/shard_map/psum | solution.py:47
  594.9 104.1 %while.14 = (s32[]{:T(128)}, f32[1024,512]{1,0:T(8,128)S(1)}, s32[32]{0:T(128)S(1)}, s32[4096]{0:T(1024)S(1)}, bf16[4096,1024]{1,0:T(8,128)(2,1)}, /*index=5*/bf...) while((s32[]{:T(128)}, f32[1024,512]{1,0:T(8,128)S(1)}, ...), condition=%wide.region_5.6_spmd.clone, body=%wide.region_4.5_spmd.clone.sunk | while | flops 203096256 | bytes 4786992 | solution.py:72
  596.2 1.9 select_add_fusion.2
  599.5 1.9 select_add_fusion.2
  606.0 1.9 select_add_fusion.2
  612.5 1.9 select_add_fusion.2
  615.8 1.9 select_add_fusion.2
  619.0 1.9 select_add_fusion.2
  625.5 1.9 select_add_fusion.2
  632.0 1.9 select_add_fusion.2
  635.3 1.9 select_add_fusion.2
  638.5 1.9 select_add_fusion.2
  645.1 1.9 select_add_fusion.2
  651.6 1.9 select_add_fusion.2
  654.8 1.9 select_add_fusion.2
  658.1 1.9 select_add_fusion.2
  664.6 1.9 select_add_fusion.2
  674.3 1.9 select_add_fusion.2
  677.6 1.9 select_add_fusion.2
  684.1 1.9 select_add_fusion.2
  (117 shorter events, 55.0 us)
Async XLA Ops:
  6.5 126.3 %copy-start = (bf16[512,1024]{1,0:T(8,128)(2,1)S(1)}, bf16[512,1024]{1,0:T(8,128)(2,1)}, u32[]{:S(2)}) copy-start(bf16[512,1024]{1,0:T(8,128)(2,1)} %param.13) | copy-start | bytes 3145732
  6.5 7.3 %copy-start.2 = (s32[4096]{0:T(1024)S(1)}, s32[4096]{0:T(1024)}, u32[]{:S(2)}) copy-start(s32[4096]{0:T(1024)} %param.8) | copy-start | bytes 49156
  6.5 113.1 %all-gather.2.cloned.1.call-start = ((), (), s32[]{:S(2)}) async-start(), calls=%async_computation.4 | async-start | bytes 8912896 | tf_op jit(solution)/shard_map/all_gather | solution.py:43
  6.5 14.8 %collective-permute-start = (bf16[32,8192]{1,0:T(8,128)(2,1)}, bf16[32,8192]{1,0:T(8,128)(2,1)S(1)}, u32[]{:S(2)}, u32[]{:S(2)}) collective-permute-start(bf16[32,8192]{1,0:T(8,128)(2,1)} %param.10), channel_id=1, source_target_pairs={{0,1},{1,2},{2,3},{3,4},{4,5},{5,6},{6,7},{7,8},{8,9},{9,10},{10,1... | collective-permute-start | bytes 1572872 | tf_op jit(solution)/shard_map/ppermute | solution.py:13
  13.8 6.3 copy-start.3
  13.8 7.5 %copy-start.6 = (bf16[32,8192]{1,0:T(8,128)(2,1)S(1)}, bf16[32,8192]{1,0:T(8,128)(2,1)}, u32[]{:S(2)}) copy-start(bf16[32,8192]{1,0:T(8,128)(2,1)} %param.10) | copy-start | bytes 1572868
  20.0 2.9 copy-start.4
  42.2 85.5 %all-to-all-start.1 = ((bf16[8,512,512]{2,1,0:T(8,128)(2,1)}), bf16[8,512,512]{2,1,0:T(8,128)(2,1)}, u32[]{:S(2)}, u32[]{:S(2)}) async-start(bf16[8,512,512]{2,1,0:T(8,128)(2,1)} %stack.5), calls=%async_computation.1 | async-start | bytes 8388608 | tf_op jit(solution)/shard_map/all_to_all | solution.py:50
  127.7 176.8 %all-to-all-start.2 = ((bf16[512,8,1024]{2,0,1:T(8,128)(2,1)}), bf16[512,8,1024]{2,0,1:T(8,128)(2,1)}, u32[]{:S(2)}, u32[]{:S(2)}) async-start(bf16[512,8,1024]{2,0,1:T(8,128)(2,1)} %bitcast.37), calls=%async_computation.2 | async-start | bytes 16777216 | tf_op jit(solution)/shard_map/all_to_all | solution.py:44
  132.7 278.0 %all-reduce.3.cloned.1.call-start = ((), (), s32[]{:S(2)}) async-start(), calls=%async_computation.3 | async-start | bytes 16777216 | tf_op jit(solution)/shard_map/psum | solution.py:55
  141.7 162.8 %copy-start.5 = (bf16[1024,512]{1,0:T(8,128)(2,1)S(1)}, bf16[1024,512]{1,0:T(8,128)(2,1)}, u32[]{:S(2)}) copy-start(bf16[1024,512]{1,0:T(8,128)(2,1)} %param.12) | copy-start | bytes 3145732
  141.8 453.1 %all-reduce.5.cloned.1.call-start = ((), (), s32[]{:S(2)}) async-start(), calls=%async_computation.5 | async-start | bytes 8388608 | tf_op jit(solution)/shard_map/psum | solution.py:47
  699.0 1.6 copy-start.1
Sparse Core Ops, SparseCore 0:
  22.9 96.6 all-gather.1
  141.9 268.8 all-reduce.2
  413.3 181.5 all-reduce.4
